TPU v7x, 128 devices: a whole 4x4x4 slice. The times are simulated.
128 devices in a mesh: dom: 32 (over x, z, core), feat: 4 (over y).
Axes of the slice: x: 4, y: 4, z: 4, core: 2. Of those that a mesh axis runs over, the one named last changes fastest.
Arguments:
- features: bfloat16 [32768, 512], P('dom'), may hold values from -96 to 96
- w_query: bfloat16 [512, 512], P(None, 'feat'), may hold values from -0.25 to 0.25
- w_key: bfloat16 [512, 512], P(None, 'feat'), may hold values from -0.25 to 0.25
- w_value: bfloat16 [512, 512], P(None, 'feat'), may hold values from -0.25 to 0.25
- cotangent: bfloat16 [32768, 512], P('dom', 'feat'), may hold values from -6 to 6
- send_rows: int32 [32, 32, 128], P('dom'), may hold values from 0 to 1023, as said below
- halo_count: int32 [32, 32], P(None, 'dom'), may hold values from 0 to 128, as said below
- block_mask: int32 [256, 40], P('dom'), may hold values 0 or 1
- exp_rows: int32 [4, 32768], P(None, 'dom'), may hold values from 0 to 1023, as said below
- global_ids: int32 [128], replicated, may hold values from 0 to 32767, as said below
Outputs:
- attended: bfloat16 [32768, 512], P('dom', 'feat')
- input_grad: bfloat16 [32768, 512], P('dom', 'feat')
Inputs may be any that keep to these rules, and one draw needn't show every extreme that they name: `send_rows`: local row numbers on the sending slab, distinct within each list. `halo_count`: zero from a slab to itself; some receiver gets 128 live slots from every other slab. `exp_rows`: each slab's part of each matching is a permutation of 0 to 1023. `global_ids`: distinct node ids.
All inputs are finite; a program needn't handle non-finite values. No bound on the sum of `block_mask` on one device may be relied on, other than what follows from the above.
Results may differ from a plain program's by a relative error of at most 0.013.
The roundings to bfloat16 on the way count: a program that leaves them out, or rounds other values in their place, can miss the bound.
Values may be sent and summed in bfloat16 or wider, within the bound.
No kernel may reach another device: no remote copies, remote signals or barrier semaphores. Data moves between devices by JAX's collectives and lax.ppermute only.
A program may use at most 128 MiB of HBM per device.

v0:
```python
import math
import jax
import jax.numpy as jnp
from jax import lax
from jax.sharding import PartitionSpec as P

HEAD = 64
BLOCK = 128
EXPANDERS = 4


def swapped_2(value, axis, bit):
    return lax.ppermute(value, axis, [(i, i ^ 1 << bit) for i in range(lax.axis_size(axis))])


def block_allowed(mask_rows, unit, key_live):
    tall = jnp.repeat(mask_rows > 0, unit, axis=0)
    return jnp.repeat(tall, unit, axis=1) & key_live[None, :]


def on_device(
    features,
    w_query,
    w_key,
    w_value,
    cotangent,
    send_rows,
    halo_count,
    block_mask,
    exp_rows,
    global_ids,
):
    node_dev = features.shape[0]
    col_count = w_query.shape[1]
    heads_here = col_count // HEAD
    dom_count = lax.axis_size("dom")
    levels = dom_count.bit_length() - 1
    my_index = lax.axis_index("dom")
    score_scale = 1.0 / math.sqrt(HEAD)
    query = jnp.dot(features, w_query, preferred_element_type=jnp.float32).astype(jnp.bfloat16)
    key_rows = jnp.dot(features, w_key, preferred_element_type=jnp.float32).astype(jnp.bfloat16)
    value_rows = jnp.dot(features, w_value, preferred_element_type=jnp.float32).astype(jnp.bfloat16)
    paired = jnp.concatenate([key_rows, value_rows], axis=1)
    outgoing = paired[send_rows[0]]
    incoming = lax.all_to_all(outgoing, "dom", split_axis=0, concat_axis=0, tiled=True)
    halo_flat = incoming.reshape(dom_count * BLOCK, 2 * col_count)
    slot_live = (jnp.arange(BLOCK, dtype=jnp.int32)[None, :] < halo_count).reshape(-1)
    key_live = jnp.concatenate([jnp.ones((node_dev,), dtype=bool), slot_live])
    cand_key = jnp.concatenate([key_rows, halo_flat[:, :col_count]], axis=0).reshape(
        -1, heads_here, HEAD
    )
    cand_value = jnp.concatenate([value_rows, halo_flat[:, col_count:]], axis=0).reshape(
        -1, heads_here, HEAD
    )
    key_total = cand_key.shape[0]
    partner_list = []
    for matching in range(EXPANDERS):
        swapped = swapped_2(paired, "dom", matching % levels)
        partner_list.append(swapped[exp_rows[matching]])
    partner_pairs = jnp.stack(partner_list)
    is_owner = global_ids // node_dev == my_index
    local_ids = global_ids % node_dev
    picked = jnp.where(is_owner[:, None], paired[local_ids].astype(jnp.float32), 0.0)
    global_pairs = lax.psum(picked.astype(jnp.bfloat16), "dom")
    global_key = global_pairs[:, :col_count].reshape(-1, heads_here, HEAD)
    global_value = global_pairs[:, col_count:].reshape(-1, heads_here, HEAD)
    rows_blk = min(256, node_dev)
    block_count = node_dev // rows_blk
    mask_blk = rows_blk // BLOCK

    def one_block(totals, block_index):
        local_gk, local_gv, global_gk, global_gv = totals
        start = block_index * rows_blk
        query_blk = lax.dynamic_slice_in_dim(query, start, rows_blk, 0).reshape(
            rows_blk, heads_here, HEAD
        )
        grad_blk = lax.dynamic_slice_in_dim(cotangent, start, rows_blk, 0).reshape(
            rows_blk, heads_here, HEAD
        )
        mask_rows = lax.dynamic_slice_in_dim(block_mask, block_index * mask_blk, mask_blk, 0)
        allowed = block_allowed(mask_rows, BLOCK, key_live)
        partner_blk = lax.dynamic_slice_in_dim(partner_pairs, start, rows_blk, 1)
        partner_key = partner_blk[..., :col_count].reshape(EXPANDERS, rows_blk, heads_here, HEAD)
        partner_value = partner_blk[..., col_count:].reshape(EXPANDERS, rows_blk, heads_here, HEAD)
        local_score = (
            jnp.einsum("rhe,khe->rhk", query_blk, cand_key, preferred_element_type=jnp.float32)
            * score_scale
        )
        local_score = jnp.where(allowed[:, None, :], local_score, -jnp.inf)
        partner_score = (
            jnp.einsum("rhe,mrhe->rhm", query_blk, partner_key, preferred_element_type=jnp.float32)
            * score_scale
        )
        global_score = (
            jnp.einsum("rhe,ghe->rhg", query_blk, global_key, preferred_element_type=jnp.float32)
            * score_scale
        )
        top_score = jnp.maximum(
            jnp.maximum(local_score.max(-1), partner_score.max(-1)), global_score.max(-1)
        )[..., None]
        local_exp = jnp.exp(local_score - top_score)
        partner_exp = jnp.exp(partner_score - top_score)
        global_exp = jnp.exp(global_score - top_score)
        denominator = (
            local_exp.sum(-1, keepdims=True)
            + partner_exp.sum(-1, keepdims=True)
            + global_exp.sum(-1, keepdims=True)
        )
        local_prob = local_exp / denominator
        partner_prob = partner_exp / denominator
        global_prob = global_exp / denominator
        local_weight = local_prob.astype(jnp.bfloat16)
        partner_weight = partner_prob.astype(jnp.bfloat16)
        global_weight = global_prob.astype(jnp.bfloat16)
        attended_blk = (
            jnp.einsum("rhk,khe->rhe", local_weight, cand_value, preferred_element_type=jnp.float32)
            + jnp.einsum(
                "rhm,mrhe->rhe", partner_weight, partner_value, preferred_element_type=jnp.float32
            )
            + jnp.einsum(
                "rhg,ghe->rhe", global_weight, global_value, preferred_element_type=jnp.float32
            )
        )
        attended_blk = attended_blk.astype(jnp.bfloat16).reshape(rows_blk, col_count)
        local_dp = jnp.einsum(
            "rhe,khe->rhk", grad_blk, cand_value, preferred_element_type=jnp.float32
        )
        partner_dp = jnp.einsum(
            "rhe,mrhe->rhm", grad_blk, partner_value, preferred_element_type=jnp.float32
        )
        global_dp = jnp.einsum(
            "rhe,ghe->rhg", grad_blk, global_value, preferred_element_type=jnp.float32
        )
        delta = (
            (local_prob * local_dp).sum(-1, keepdims=True)
            + (partner_prob * partner_dp).sum(-1, keepdims=True)
            + (global_prob * global_dp).sum(-1, keepdims=True)
        )
        local_ds = (local_prob * (local_dp - delta) * score_scale).astype(jnp.bfloat16)
        partner_ds = (partner_prob * (partner_dp - delta) * score_scale).astype(jnp.bfloat16)
        global_ds = (global_prob * (global_dp - delta) * score_scale).astype(jnp.bfloat16)
        grad_query_blk = (
            jnp.einsum("rhk,khe->rhe", local_ds, cand_key, preferred_element_type=jnp.float32)
            + jnp.einsum(
                "rhm,mrhe->rhe", partner_ds, partner_key, preferred_element_type=jnp.float32
            )
            + jnp.einsum("rhg,ghe->rhe", global_ds, global_key, preferred_element_type=jnp.float32)
        )
        local_gk = local_gk + jnp.einsum(
            "rhk,rhe->khe", local_ds, query_blk, preferred_element_type=jnp.float32
        )
        local_gv = local_gv + jnp.einsum(
            "rhk,rhe->khe", local_weight, grad_blk, preferred_element_type=jnp.float32
        )
        global_gk = global_gk + jnp.einsum(
            "rhg,rhe->ghe", global_ds, query_blk, preferred_element_type=jnp.float32
        )
        global_gv = global_gv + jnp.einsum(
            "rhg,rhe->ghe", global_weight, grad_blk, preferred_element_type=jnp.float32
        )
        return (
            (local_gk, local_gv, global_gk, global_gv),
            (attended_blk, grad_query_blk.reshape(rows_blk, col_count), partner_ds, partner_weight),
        )

    zero_keys = jnp.zeros((key_total, heads_here, HEAD), jnp.float32)
    zero_globals = jnp.zeros((global_ids.shape[0], heads_here, HEAD), jnp.float32)
    totals, outputs = lax.scan(
        one_block, (zero_keys, zero_keys, zero_globals, zero_globals), jnp.arange(block_count)
    )
    local_gk, local_gv, global_gk, global_gv = totals
    attended_rows, grad_query, partner_ds, partner_weight = outputs
    attended = attended_rows.reshape(node_dev, col_count)
    grad_query = grad_query.reshape(node_dev, col_count)
    partner_ds = partner_ds.reshape(node_dev, heads_here, EXPANDERS)
    partner_weight = partner_weight.reshape(node_dev, heads_here, EXPANDERS)
    key_grads = local_gk.reshape(key_total, col_count)
    value_grads = local_gv.reshape(key_total, col_count)
    pair_grad = jnp.concatenate([key_grads[:node_dev], value_grads[:node_dev]], axis=1)
    halo_back = jnp.concatenate([key_grads[node_dev:], value_grads[node_dev:]], axis=1).reshape(
        dom_count, BLOCK, 2 * col_count
    )
    returned = lax.all_to_all(
        halo_back.astype(jnp.bfloat16), "dom", split_axis=0, concat_axis=0, tiled=True
    )
    pair_grad = pair_grad.at[send_rows[0].reshape(-1)].add(
        returned.reshape(-1, 2 * col_count).astype(jnp.float32)
    )
    for matching in range(EXPANDERS):
        bit_level = matching % levels
        row_order = exp_rows[matching]
        key_term = partner_ds[:, :, matching, None].astype(jnp.float32) * query.reshape(
            node_dev, heads_here, HEAD
        ).astype(jnp.float32)
        value_term = partner_weight[:, :, matching, None].astype(jnp.float32) * cotangent.reshape(
            node_dev, heads_here, HEAD
        ).astype(jnp.float32)
        joined = jnp.concatenate(
            [key_term.reshape(node_dev, col_count), value_term.reshape(node_dev, col_count)], axis=1
        )
        placed = jnp.zeros_like(joined).at[row_order].set(joined)
        pair_grad = pair_grad + swapped_2(placed.astype(jnp.bfloat16), "dom", bit_level).astype(
            placed.dtype
        )
    global_grad = jnp.concatenate(
        [global_gk.reshape(-1, col_count), global_gv.reshape(-1, col_count)], axis=1
    )
    summed = lax.psum(global_grad.astype(jnp.bfloat16), "dom").astype(jnp.float32)
    pair_grad = pair_grad.at[local_ids].add(jnp.where(is_owner[:, None], summed, 0.0))
    feature_terms = (
        jnp.dot(grad_query.astype(jnp.bfloat16), w_query.T, preferred_element_type=jnp.float32)
        + jnp.dot(
            pair_grad[:, :col_count].astype(jnp.bfloat16),
            w_key.T,
            preferred_element_type=jnp.float32,
        )
        + jnp.dot(
            pair_grad[:, col_count:].astype(jnp.bfloat16),
            w_value.T,
            preferred_element_type=jnp.float32,
        )
    )
    input_grad = lax.psum_scatter(feature_terms, "feat", scatter_dimension=1, tiled=True).astype(
        jnp.bfloat16
    )
    return (attended, input_grad)


def solution(mesh):
    return jax.shard_map(
        on_device,
        mesh=mesh,
        in_specs=(
            P("dom", None),
            P(None, "feat"),
            P(None, "feat"),
            P(None, "feat"),
            P("dom", "feat"),
            P("dom", None, None),
            P(None, "dom"),
            P("dom", None),
            P(None, "dom"),
            P(),
        ),
        out_specs=(P("dom", "feat"), P("dom", "feat")),
        check_vma=False,
    )
```

profile of v0, /device:TPU:1, one launch (start us, length us, event | category | flops | bytes accessed | tf_op | source)
XLA Modules:
  0.0 586.4 jit_solution(14606089419128119162)
XLA Ops:
  19.1 17.0 %gather_fusion = bf16[4096,256]{1,0:T(8,128)(2,1)} fusion(bf16[1024,256]{1,0:T(8,128)(2,1)S(1)} %pad_maximum_fusion.8, s32[4096]{0:T(1024)S(1)} %fusion.59), kind=kCustom, calls=%fused_computation | custom fusion | bytes 4210688 | tf_op jit(solution)/shard_map/gather | solution.py:44
  36.1 5.1 all-to-all-start
  54.5 93.9 %all-reduce.4.cloned.1.call-done = bf16[128,256]{1,0:T(8,128)(2,1)} async-done(((bf16[128,256]{1,0:T(8,128)(2,1)}), bf16[128,256]{1,0:T(8,128)(2,1)}) %all-reduce.4.cloned.1.call-update) | async-done | bytes 65552 | tf_op jit(solution)/shard_map/psum | solution.py:64
  182.1 211.5 %while.25 = (s32[]{:T(128)}, f32[5120,2,64]{0,2,1:T(8,128)}, f32[5120,2,64]{0,2,1:T(8,128)}, f32[128,2,64]{0,2,1:T(8,128)}, f32[128,2,64]{0,2,1:T(8,128)}, /*ind...) while((s32[]{:T(128)}, f32[5120,2,64]{0,2,1:T(8,128)}, ...), condition=%wide.region_11.12_spmd.clone, body=%wide.region_1.11_spmd.clone.sunk | while | flops 2151969280 | bytes 260182544 | solution.py:168
  203.6 8.3 %fusion.169 = f32[5120,2,64]{0,2,1:T(8,128)} fusion(bf16[256,2,64]{0,2,1:T(8,128)(2,1)S(1)} %bitcast.353, f32[5120,2,64]{0,2,1:T(8,128)} %get-tuple-element.548, pred[]{:T(512)S(6)} %compare.7, f32[2,256,5120]{2,1,0:T(8,128)} %copy-done.2, f32[256,2]{0,1:T(2,128)S(1)} %add_add_fusion.5, f32[256,2]{0,1:T(2,128)S(1)} %maximum_maximum_fusion.2, ...), kind=kOutput, calls=%fused_computation.25.clone.1 | convolution fusion | flops 349962240 | bytes 17108992 | tf_op jit(solution)/shard_map/while/body/eval_jaxpr/rhk,rhe->khe/dot_general | solution.py:152
  212.0 7.3 %fusion.166 = (f32[256,2]{0,1:T(2,128)S(1)}, f32[2,256,5120]{2,1,0:T(8,128)}) fusion(f32[256,2]{0,1:T(2,128)S(1)} %add_add_fusion.5, f32[256,2]{0,1:T(2,128)S(1)} %maximum_maximum_fusion.2, f32[2,256,5120]{2,1,0:T(8,128)S(1)} %bitcast.324, pred[256,5120]{1,0:T(8,128)(4,1)S(1)} %bitcast_and_fusion.2, bf16[256,2,64]{0,2,1:T(8,128)(2,1)S(1)} %bitcast.354, ...), kind=kOutput, calls=%fused_computation.14.clone.1 | convolution fusion | flops 351272448 | bytes 23664640 | tf_op jit(solution)/shard_map/while/body/eval_jaxpr/rhe,khe->rhk/dot_general | solution.py:125
  219.4 7.1 %fusion.167 = bf16[256,2,5120]{2,0,1:T(8,128)(2,1)S(1)} fusion(f32[2,256,5120]{2,1,0:T(8,128)} %get-tuple-element.506, f32[256,2]{0,1:T(2,128)S(1)} %add_add_fusion.6, f32[256,2]{0,1:T(2,128)S(1)} %add_add_fusion.5, f32[256,2]{0,1:T(2,128)S(1)} %maximum_maximum_fusion.2, f32[2,256,5120]{2,1,0:T(8,128)S(1)} %bitcast.324, ...), kind=kLoop, calls=%fused_computation.17.clone.1 | loop fusion | flops 20971520 | bytes 27531264 | tf_op jit(solution)/shard_map/while/body/eval_jaxpr/convert_element_type | solution.py:139
  256.0 9.1 %fusion.169 = f32[5120,2,64]{0,2,1:T(8,128)} fusion(bf16[256,2,64]{0,2,1:T(8,128)(2,1)S(1)} %bitcast.353, f32[5120,2,64]{0,2,1:T(8,128)} %get-tuple-element.548, pred[]{:T(512)S(6)} %compare.7, f32[2,256,5120]{2,1,0:T(8,128)} %copy-done.2, f32[256,2]{0,1:T(2,128)S(1)} %add_add_fusion.5, f32[256,2]{0,1:T(2,128)S(1)} %maximum_maximum_fusion.2, ...), kind=kOutput, calls=%fused_computation.25.clone.1 | convolution fusion | flops 349962240 | bytes 17108992 | tf_op jit(solution)/shard_map/while/body/eval_jaxpr/rhk,rhe->khe/dot_general | solution.py:152
  265.1 7.3 %fusion.166 = (f32[256,2]{0,1:T(2,128)S(1)}, f32[2,256,5120]{2,1,0:T(8,128)}) fusion(f32[256,2]{0,1:T(2,128)S(1)} %add_add_fusion.5, f32[256,2]{0,1:T(2,128)S(1)} %maximum_maximum_fusion.2, f32[2,256,5120]{2,1,0:T(8,128)S(1)} %bitcast.324, pred[256,5120]{1,0:T(8,128)(4,1)S(1)} %bitcast_and_fusion.2, bf16[256,2,64]{0,2,1:T(8,128)(2,1)S(1)} %bitcast.354, ...), kind=kOutput, calls=%fused_computation.14.clone.1 | convolution fusion | flops 351272448 | bytes 23664640 | tf_op jit(solution)/shard_map/while/body/eval_jaxpr/rhe,khe->rhk/dot_general | solution.py:125
  272.6 7.1 %fusion.167 = bf16[256,2,5120]{2,0,1:T(8,128)(2,1)S(1)} fusion(f32[2,256,5120]{2,1,0:T(8,128)} %get-tuple-element.506, f32[256,2]{0,1:T(2,128)S(1)} %add_add_fusion.6, f32[256,2]{0,1:T(2,128)S(1)} %add_add_fusion.5, f32[256,2]{0,1:T(2,128)S(1)} %maximum_maximum_fusion.2, f32[2,256,5120]{2,1,0:T(8,128)S(1)} %bitcast.324, ...), kind=kLoop, calls=%fused_computation.17.clone.1 | loop fusion | flops 20971520 | bytes 27531264 | tf_op jit(solution)/shard_map/while/body/eval_jaxpr/convert_element_type | solution.py:139
  309.2 9.1 %fusion.169 = f32[5120,2,64]{0,2,1:T(8,128)} fusion(bf16[256,2,64]{0,2,1:T(8,128)(2,1)S(1)} %bitcast.353, f32[5120,2,64]{0,2,1:T(8,128)} %get-tuple-element.548, pred[]{:T(512)S(6)} %compare.7, f32[2,256,5120]{2,1,0:T(8,128)} %copy-done.2, f32[256,2]{0,1:T(2,128)S(1)} %add_add_fusion.5, f32[256,2]{0,1:T(2,128)S(1)} %maximum_maximum_fusion.2, ...), kind=kOutput, calls=%fused_computation.25.clone.1 | convolution fusion | flops 349962240 | bytes 17108992 | tf_op jit(solution)/shard_map/while/body/eval_jaxpr/rhk,rhe->khe/dot_general | solution.py:152
  318.4 7.3 %fusion.166 = (f32[256,2]{0,1:T(2,128)S(1)}, f32[2,256,5120]{2,1,0:T(8,128)}) fusion(f32[256,2]{0,1:T(2,128)S(1)} %add_add_fusion.5, f32[256,2]{0,1:T(2,128)S(1)} %maximum_maximum_fusion.2, f32[2,256,5120]{2,1,0:T(8,128)S(1)} %bitcast.324, pred[256,5120]{1,0:T(8,128)(4,1)S(1)} %bitcast_and_fusion.2, bf16[256,2,64]{0,2,1:T(8,128)(2,1)S(1)} %bitcast.354, ...), kind=kOutput, calls=%fused_computation.14.clone.1 | convolution fusion | flops 351272448 | bytes 23664640 | tf_op jit(solution)/shard_map/while/body/eval_jaxpr/rhe,khe->rhk/dot_general | solution.py:125
  325.8 7.1 %fusion.167 = bf16[256,2,5120]{2,0,1:T(8,128)(2,1)S(1)} fusion(f32[2,256,5120]{2,1,0:T(8,128)} %get-tuple-element.506, f32[256,2]{0,1:T(2,128)S(1)} %add_add_fusion.6, f32[256,2]{0,1:T(2,128)S(1)} %add_add_fusion.5, f32[256,2]{0,1:T(2,128)S(1)} %maximum_maximum_fusion.2, f32[2,256,5120]{2,1,0:T(8,128)S(1)} %bitcast.324, ...), kind=kLoop, calls=%fused_computation.17.clone.1 | loop fusion | flops 20971520 | bytes 27531264 | tf_op jit(solution)/shard_map/while/body/eval_jaxpr/convert_element_type | solution.py:139
  362.3 9.1 %fusion.169 = f32[5120,2,64]{0,2,1:T(8,128)} fusion(bf16[256,2,64]{0,2,1:T(8,128)(2,1)S(1)} %bitcast.353, f32[5120,2,64]{0,2,1:T(8,128)} %get-tuple-element.548, pred[]{:T(512)S(6)} %compare.7, f32[2,256,5120]{2,1,0:T(8,128)} %copy-done.2, f32[256,2]{0,1:T(2,128)S(1)} %add_add_fusion.5, f32[256,2]{0,1:T(2,128)S(1)} %maximum_maximum_fusion.2, ...), kind=kOutput, calls=%fused_computation.25.clone.1 | convolution fusion | flops 349962240 | bytes 17108992 | tf_op jit(solution)/shard_map/while/body/eval_jaxpr/rhk,rhe->khe/dot_general | solution.py:152
  371.5 7.3 %fusion.166 = (f32[256,2]{0,1:T(2,128)S(1)}, f32[2,256,5120]{2,1,0:T(8,128)}) fusion(f32[256,2]{0,1:T(2,128)S(1)} %add_add_fusion.5, f32[256,2]{0,1:T(2,128)S(1)} %maximum_maximum_fusion.2, f32[2,256,5120]{2,1,0:T(8,128)S(1)} %bitcast.324, pred[256,5120]{1,0:T(8,128)(4,1)S(1)} %bitcast_and_fusion.2, bf16[256,2,64]{0,2,1:T(8,128)(2,1)S(1)} %bitcast.354, ...), kind=kOutput, calls=%fused_computation.14.clone.1 | convolution fusion | flops 351272448 | bytes 23664640 | tf_op jit(solution)/shard_map/while/body/eval_jaxpr/rhe,khe->rhk/dot_general | solution.py:125
  378.9 7.1 %fusion.167 = bf16[256,2,5120]{2,0,1:T(8,128)(2,1)S(1)} fusion(f32[2,256,5120]{2,1,0:T(8,128)} %get-tuple-element.506, f32[256,2]{0,1:T(2,128)S(1)} %add_add_fusion.6, f32[256,2]{0,1:T(2,128)S(1)} %add_add_fusion.5, f32[256,2]{0,1:T(2,128)S(1)} %maximum_maximum_fusion.2, f32[2,256,5120]{2,1,0:T(8,128)S(1)} %bitcast.324, ...), kind=kLoop, calls=%fused_computation.17.clone.1 | loop fusion | flops 20971520 | bytes 27531264 | tf_op jit(solution)/shard_map/while/body/eval_jaxpr/convert_element_type | solution.py:139
  410.4 5.5 scatter_custom_fusion
  419.3 5.5 scatter_custom_fusion.1
  427.1 5.5 scatter_custom_fusion.2
  433.9 5.4 scatter_custom_fusion.3
  456.2 11.4 %collective-permute-done.5 = bf16[1024,256]{1,0:T(8,128)(2,1)} collective-permute-done((bf16[1024,256]{1,0:T(8,128)(2,1)}, bf16[1024,256]{1,0:T(8,128)(2,1)}, u32[]{:S(2)}, u32[]{:S(2)}) %collective-permute-start.5) | collective-permute-done | bytes 524320 | tf_op jit(solution)/shard_map/ppermute | solution.py:13
  473.5 23.4 %scatter_custom_fusion.4 = f32[1024,256]{1,0:T(8,128)S(1)} fusion(f32[1024,256]{1,0:T(8,128)S(1)} %fusion.41, s32[4096]{0:T(1024)S(1)} %bitcast.365, bf16[4096,256]{1,0:T(8,128)(2,1)} %bitcast.333), kind=kCustom, calls=%fused_computation.82 | custom fusion | flops 2097152 | bytes 3145728 | tf_op jit(solution)/shard_map/scatter-add | solution.py:186
  497.0 48.0 %all-reduce.6.cloned.1.call-done = bf16[128,256]{1,0:T(8,128)(2,1)} async-done(((bf16[128,256]{1,0:T(8,128)(2,1)}), bf16[128,256]{1,0:T(8,128)(2,1)}) %all-reduce.6.cloned.1.call-update) | async-done | bytes 65552 | tf_op jit(solution)/shard_map/psum | solution.py:208
  549.5 28.4 %reduce-scatter.2.cloned.1.call-done = f32[1024,128]{1,0:T(8,128)} async-done(((f32[1024,512]{1,0:T(8,128)}), f32[1024,128]{1,0:T(8,128)}) %reduce-scatter.2.cloned.1.call-update) | async-done | bytes 524304 | tf_op jit(solution)/shard_map/reduce_scatter | solution.py:223
  (468 shorter events, 222.1 us)
Async XLA Ops:
  7.2 11.9 %copy-start.27 = (s32[1,32,128]{2,1,0:T(8,128)S(1)}, s32[1,32,128]{2,1,0:T(8,128)}, u32[]{:S(2)}) copy-start(s32[1,32,128]{2,1,0:T(8,128)} %param.17) | copy-start | bytes 49156
  11.2 139.4 %collective-permute-start.3 = (bf16[1024,256]{1,0:T(8,128)(2,1)S(1)}, bf16[1024,256]{1,0:T(8,128)(2,1)}, u32[]{:S(2)}, u32[]{:S(2)}) collective-permute-start(bf16[1024,256]{1,0:T(8,128)(2,1)S(1)} %pad_maximum_fusion.8), channel_id=1, source_target_pairs={{0,32},{4,36},{8,40},{12,44},{16,48},{20,52},{24,56},{28,60},{32,0... | collective-permute-start | bytes 1572872 | tf_op jit(solution)/shard_map/ppermute | solution.py:13
  13.3 142.4 %collective-permute-start.2 = (bf16[1024,256]{1,0:T(8,128)(2,1)S(1)}, bf16[1024,256]{1,0:T(8,128)(2,1)S(1)}, u32[]{:S(2)}, u32[]{:S(2)}) collective-permute-start(bf16[1024,256]{1,0:T(8,128)(2,1)S(1)} %pad_maximum_fusion.8), channel_id=1, source_target_pairs={{0,16},{4,20},{8,24},{12,28},{16,0},{20,4},{24,8},{28,12},{32,48},... | collective-permute-start | bytes 1572872 | tf_op jit(solution)/shard_map/ppermute | solution.py:13
  16.9 142.8 %collective-permute-start.1 = (bf16[1024,256]{1,0:T(8,128)(2,1)S(1)}, bf16[1024,256]{1,0:T(8,128)(2,1)S(1)}, u32[]{:S(2)}, u32[]{:S(2)}) collective-permute-start(bf16[1024,256]{1,0:T(8,128)(2,1)S(1)} %pad_maximum_fusion.8), channel_id=1, source_target_pairs={{0,8},{4,12},{8,0},{12,4},{16,24},{20,28},{24,16},{28,20},{32,40},... | collective-permute-start | bytes 1572872 | tf_op jit(solution)/shard_map/ppermute | solution.py:13
  17.6 147.0 %collective-permute-start = (bf16[1024,256]{1,0:T(8,128)(2,1)S(1)}, bf16[1024,256]{1,0:T(8,128)(2,1)S(1)}, u32[]{:S(2)}, u32[]{:S(2)}) collective-permute-start(bf16[1024,256]{1,0:T(8,128)(2,1)S(1)} %pad_maximum_fusion.8), channel_id=1, source_target_pairs={{0,4},{4,0},{8,12},{12,8},{16,20},{20,16},{24,28},{28,24},{32,36},... | collective-permute-start | bytes 1572872 | tf_op jit(solution)/shard_map/ppermute | solution.py:13
  36.1 12.0 %copy-start.22 = (bf16[512,128]{1,0:T(8,128)(2,1)S(1)}, bf16[512,128]{1,0:T(8,128)(2,1)}, u32[]{:S(2)}) copy-start(bf16[512,128]{1,0:T(8,128)(2,1)} %param.13) | copy-start | bytes 393220
  36.1 134.9 %all-to-all-start = ((bf16[32,128,256]{2,1,0:T(8,128)(2,1)}), bf16[32,128,256]{2,1,0:T(8,128)(2,1)}, u32[]{:S(2)}, u32[]{:S(2)}) async-start(bf16[32,128,256]{2,1,0:T(8,128)(2,1)} %bitcast.334), calls=%async_computation | async-start | bytes 4194304 | tf_op jit(solution)/shard_map/all_to_all | solution.py:45
  41.2 107.2 %all-reduce.4.cloned.1.call-start = ((), (), s32[]{:S(2)}) async-start(), calls=%async_computation.3 | async-start | bytes 131072 | tf_op jit(solution)/shard_map/psum | solution.py:64
  401.4 68.1 %all-to-all-start.1 = ((bf16[32,128,256]{1,2,0:T(8,128)(2,1)}), bf16[32,128,256]{1,2,0:T(8,128)(2,1)}, u32[]{:S(2)}, u32[]{:S(2)}) async-start(bf16[32,128,256]{1,2,0:T(8,128)(2,1)} %copy.127), calls=%async_computation.1 | async-start | bytes 4194304 | tf_op jit(solution)/shard_map/all_to_all | solution.py:183
  406.4 138.6 %all-reduce.6.cloned.1.call-start = ((), (), s32[]{:S(2)}) async-start(), calls=%async_computation.4 | async-start | bytes 131072 | tf_op jit(solution)/shard_map/psum | solution.py:208
  433.5 12.2 %copy-start.28 = (s32[1,32,128]{2,1,0:T(8,128)S(1)}, s32[1,32,128]{2,1,0:T(8,128)}, u32[]{:S(2)}) copy-start(s32[1,32,128]{2,1,0:T(8,128)} %param.17) | copy-start | bytes 49156
  433.9 14.1 %copy-start.15 = (f32[128,2,64]{0,2,1:T(8,128)S(1)}, f32[128,2,64]{0,2,1:T(8,128)}, u32[]{:S(2)}) copy-start(f32[128,2,64]{0,2,1:T(8,128)} %get-tuple-element.642) | copy-start | bytes 196612
  440.2 11.7 %copy-start.26 = (bf16[4,256,128]{2,1,0:T(8,128)(2,1)S(1)}, bf16[4,256,128]{2,1,0:T(8,128)(2,1)}, u32[]{:S(2)}) copy-start(bf16[4,256,128]{2,1,0:T(8,128)(2,1)} %get-tuple-element.645) | copy-start | bytes 786436
  440.2 13.5 %collective-permute-start.7 = (bf16[1024,256]{1,0:T(8,128)(2,1)}, bf16[1024,256]{1,0:T(8,128)(2,1)}, u32[]{:S(2)}, u32[]{:S(2)}) collective-permute-start(bf16[1024,256]{1,0:T(8,128)(2,1)} %convert_element_type.125), channel_id=1, source_target_pairs={{0,32},{4,36},{8,40},{12,44},{16,48},{20,52},{24,56},{28,60},{32,0... | collective-permute-start | bytes 1572872 | tf_op jit(solution)/shard_map/ppermute | solution.py:13
  441.6 14.7 %collective-permute-start.6 = (bf16[1024,256]{1,0:T(8,128)(2,1)}, bf16[1024,256]{1,0:T(8,128)(2,1)}, u32[]{:S(2)}, u32[]{:S(2)}) collective-permute-start(bf16[1024,256]{1,0:T(8,128)(2,1)} %convert_element_type.123), channel_id=1, source_target_pairs={{0,16},{4,20},{8,24},{12,28},{16,0},{20,4},{24,8},{28,12},{32,48},... | collective-permute-start | bytes 1572872 | tf_op jit(solution)/shard_map/ppermute | solution.py:13
  444.3 23.3 %collective-permute-start.5 = (bf16[1024,256]{1,0:T(8,128)(2,1)}, bf16[1024,256]{1,0:T(8,128)(2,1)}, u32[]{:S(2)}, u32[]{:S(2)}) collective-permute-start(bf16[1024,256]{1,0:T(8,128)(2,1)} %convert_element_type.121), channel_id=1, source_target_pairs={{0,8},{4,12},{8,0},{12,4},{16,24},{20,28},{24,16},{28,20},{32,40},... | collective-permute-start | bytes 1572872 | tf_op jit(solution)/shard_map/ppermute | solution.py:13
  444.6 23.0 %collective-permute-start.4 = (bf16[1024,256]{1,0:T(8,128)(2,1)}, bf16[1024,256]{1,0:T(8,128)(2,1)}, u32[]{:S(2)}, u32[]{:S(2)}) collective-permute-start(bf16[1024,256]{1,0:T(8,128)(2,1)} %convert_element_type.119), channel_id=1, source_target_pairs={{0,4},{4,0},{8,12},{12,8},{16,20},{20,16},{24,28},{28,24},{32,36},... | collective-permute-start | bytes 1572872 | tf_op jit(solution)/shard_map/ppermute | solution.py:13
  449.7 128.2 %reduce-scatter.2.cloned.1.call-start = ((), (), s32[]{:S(2)}) async-start(), calls=%async_computation.5 | async-start | bytes 2621440 | tf_op jit(solution)/shard_map/reduce_scatter | solution.py:223
  451.9 15.7 %copy-start.18 = (f32[1024,128]{1,0:T(8,128)S(1)}, f32[1024,128]{1,0:T(8,128)}, u32[]{:S(2)}) copy-start(f32[1024,128]{1,0:T(8,128)} %copy.118) | copy-start | bytes 1572868
  451.9 15.7 %copy-start.19 = (f32[1024,128]{1,0:T(8,128)S(1)}, f32[1024,128]{1,0:T(8,128)}, u32[]{:S(2)}) copy-start(f32[1024,128]{1,0:T(8,128)} %copy.119) | copy-start | bytes 1572868
  473.5 71.5 %copy-start.35 = (pred[128]{0:T(512)(128)(4,1)S(1)}, pred[128]{0:T(512)(128)(4,1)}, u32[]{:S(2)}) copy-start(pred[128]{0:T(512)(128)(4,1)} %fusion.61) | copy-start | bytes 388
  473.5 73.6 %copy-start.24 = (bf16[512,128]{1,0:T(8,128)(2,1)S(1)}, bf16[512,128]{1,0:T(8,128)(2,1)}, u32[]{:S(2)}) copy-start(bf16[512,128]{1,0:T(8,128)(2,1)} %param.14) | copy-start | bytes 393220
  497.0 50.6 %copy-start.25 = (bf16[512,128]{1,0:T(8,128)(2,1)S(1)}, bf16[512,128]{1,0:T(8,128)(2,1)}, u32[]{:S(2)}) copy-start(bf16[512,128]{1,0:T(8,128)(2,1)} %param.15) | copy-start | bytes 393220
  547.6 32.1 %copy-start.1 = (bf16[1024,512]{1,0:T(8,128)(2,1)S(1)}, bf16[1024,512]{1,0:T(8,128)(2,1)}, u32[]{:S(2)}) copy-start(bf16[1024,512]{1,0:T(8,128)(2,1)} %param.12) | copy-start | bytes 3145732
  (85 other events, 437.4 us)
Sparse Core Ops, SparseCore 0:
  46.9 101.4 all-reduce.3
  449.9 95.0 all-reduce.5
  549.6 28.2 reduce-scatter.1
where the time goes:
time: 594 us; the launch traced here: 586 us
  waiting for transfers between devices  186 us (31%)
  matrix products  128 us (22%)
  local copies, waits for them, and re-layouts  118 us (20%)
  other arithmetic  109 us (18%)
  starting transfers between devices  23.7 us (4%)
  between operations  14.5 us (2%)
  loops' own time  7.29 us (1%)
    psum x1, waiting for transfers between devices, on_device(): global_pairs = lax.psum(picked.astype(jnp.bfloat16), 'dom')  93.9 us
    psum x1, waiting for transfers between devices, on_device(): lax.psum(global_grad.astype(jnp.bfloat16), 'dom').astype(jnp.float32)  48 us
    dot_general x4, matrix products, one_block(): jnp.einsum('rhk,rhe->khe', local_weight, grad_blk, preferred_element_type...  35.7 us
    dot_general x4, matrix products, one_block(): jnp.einsum('rhe,khe->rhk', grad_blk, cand_value, preferred_element_type=j...  29.3 us
    reduce_scatter x1, waiting for transfers between devices, on_device(): lax.psum_scatter(feature_terms, 'feat', scatter_dimension=1, tiled=True)  28.4 us
    convert_element_type x4, other arithmetic, one_block(): (local_prob * (local_dp - delta) * score_scale).astype(jnp.bfloat16)  28.3 us
    scatter-add x1, other arithmetic, on_device(): pair_grad.at[send_rows[0].reshape(-1)]  23.4 us
    scatter x4, local copies, waits for them, and re-layouts, on_device(): placed = jnp.zeros_like(joined).at[row_order].set(joined)  22 us
  transfers between devices with their start and end apart: 13, of which 6 were waited for; matrix products, arithmetic and copies ran while one was open for 21% of the time, Pallas kernels for 0%

commit v1 on v0

--- a/solution.py
+++ b/solution.py
@@ -61,7 +61,9 @@
     is_owner = global_ids // node_dev == my_index
     local_ids = global_ids % node_dev
     picked = jnp.where(is_owner[:, None], paired[local_ids].astype(jnp.float32), 0.0)
-    global_pairs = lax.psum(picked.astype(jnp.bfloat16), "dom")
+    x = picked.astype(jnp.bfloat16)
+    parts = lax.all_gather(x, "dom")
+    global_pairs = jnp.sum(parts, axis=0)
     global_key = global_pairs[:, :col_count].reshape(-1, heads_here, HEAD)
     global_value = global_pairs[:, col_count:].reshape(-1, heads_here, HEAD)
     rows_blk = min(256, node_dev)

time: 594 us -> 530 us (0.89)
  waiting for transfers between devices: 186 us -> 115 us
    psum x1 -> x0, waiting for transfers between devices: 93.9 us -> none  [on_device(): global_pairs = lax.psum(picked.astype(jnp.bfloat16), 'dom')]
    ppermute x8, waiting for transfers between devices: 15.3 us -> 37.9 us  [swapped_2(): lax.ppermute(value, axis, [(i, i ^ 1 << bit) for i in range(lax.axis_size...]
  transfers between devices with their start and end apart: 13 -> 13, of which waited for: 6 -> 7; matrix products, arithmetic and copies ran while one was open for 21% -> 21% of each run, Pallas kernels for 0% -> 0%
where the time goes in v1:
time: 530 us; the launch traced here: 521 us
  matrix products  131 us (25%)
  local copies, waits for them, and re-layouts  116 us (22%)
  waiting for transfers between devices  115 us (22%)
  other arithmetic  109 us (21%)
  starting transfers between devices  28.3 us (5%)
  between operations  14.5 us (3%)
  loops' own time  7.21 us (1%)
    psum x1, waiting for transfers between devices, on_device(): lax.psum(global_grad.astype(jnp.bfloat16), 'dom').astype(jnp.float32)  48.2 us
    ppermute x8, waiting for transfers between devices, swapped_2(): lax.ppermute(value, axis, [(i, i ^ 1 << bit) for i in range(lax.axis_size...  37.9 us
    dot_general x4, matrix products, one_block(): jnp.einsum('rhk,rhe->khe', local_weight, grad_blk, preferred_element_type...  35.7 us
    dot_general x4, matrix products, one_block(): jnp.einsum('rhe,khe->rhk', grad_blk, cand_value, preferred_element_type=j...  29.3 us
    reduce_scatter x1, waiting for transfers between devices, on_device(): lax.psum_scatter(feature_terms, 'feat', scatter_dimension=1, tiled=True)  28.4 us
    convert_element_type x4, other arithmetic, one_block(): (local_prob * (local_dp - delta) * score_scale).astype(jnp.bfloat16)  28.3 us
    scatter-add x1, other arithmetic, on_device(): pair_grad.at[send_rows[0].reshape(-1)]  23.4 us
    scatter x4, local copies, waits for them, and re-layouts, on_device(): placed = jnp.zeros_like(joined).at[row_order].set(joined)  22 us
  transfers between devices with their start and end apart: 13, of which 7 were waited for; matrix products, arithmetic and copies ran while one was open for 21% of the time, Pallas kernels for 0%

profile of v1, /device:TPU:1, one launch (start us, length us, event | category | flops | bytes accessed | tf_op | source)
XLA Modules:
  0.0 521.2 jit_solution(17090711080600719638)
XLA Ops:
  11.2 16.9 %gather_fusion = bf16[4096,256]{1,0:T(8,128)(2,1)} fusion(bf16[1024,256]{1,0:T(8,128)(2,1)S(1)} %pad_maximum_fusion.8, s32[4096]{0:T(1024)S(1)} %fusion.60), kind=kCustom, calls=%fused_computation | custom fusion | bytes 4210688 | tf_op jit(solution)/shard_map/gather | solution.py:44
  28.1 9.6 %all-to-all-start = ((bf16[32,128,256]{2,1,0:T(8,128)(2,1)}), bf16[32,128,256]{2,1,0:T(8,128)(2,1)}, u32[]{:S(2)}, u32[]{:S(2)}) async-start(bf16[32,128,256]{2,1,0:T(8,128)(2,1)} %bitcast.337), calls=%async_computation | async-start | bytes 4194304 | tf_op jit(solution)/shard_map/all_to_all | solution.py:45
  54.4 20.6 %collective-permute-done.3 = bf16[1024,256]{1,0:T(8,128)(2,1)} collective-permute-done((bf16[1024,256]{1,0:T(8,128)(2,1)S(1)}, bf16[1024,256]{1,0:T(8,128)(2,1)}, u32[]{:S(2)}, u32[]{:S(2)}) %collective-permute-start.3) | collective-permute-done | bytes 524320 | tf_op jit(solution)/shard_map/ppermute | solution.py:13
  111.4 214.5 %while.25 = (s32[]{:T(128)}, f32[5120,2,64]{0,2,1:T(8,128)}, f32[5120,2,64]{0,2,1:T(8,128)}, f32[128,2,64]{0,2,1:T(8,128)}, f32[128,2,64]{0,2,1:T(8,128)}, /*ind...) while((s32[]{:T(128)}, f32[5120,2,64]{0,2,1:T(8,128)}, ...), condition=%wide.region_11.12_spmd.clone, body=%wide.region_1.11_spmd.clone.sunk | while | flops 2151969280 | bytes 260051440 | solution.py:170
  133.7 8.3 %fusion.170 = f32[5120,2,64]{0,2,1:T(8,128)} fusion(bf16[256,2,64]{0,2,1:T(8,128)(2,1)S(1)} %bitcast.353, f32[5120,2,64]{0,2,1:T(8,128)} %get-tuple-element.548, pred[]{:T(512)S(6)} %compare.7, f32[2,256,5120]{2,1,0:T(8,128)} %copy-done.2, f32[256,2]{0,1:T(2,128)S(1)} %add_add_fusion.5, f32[256,2]{0,1:T(2,128)S(1)} %maximum_maximum_fusion.2, ...), kind=kOutput, calls=%fused_computation.25.clone.1 | convolution fusion | flops 349962240 | bytes 17108992 | tf_op jit(solution)/shard_map/while/body/eval_jaxpr/rhk,rhe->khe/dot_general | solution.py:154
  142.0 7.3 %fusion.167 = (f32[256,2]{0,1:T(2,128)S(1)}, f32[2,256,5120]{2,1,0:T(8,128)}) fusion(f32[256,2]{0,1:T(2,128)S(1)} %add_add_fusion.5, f32[256,2]{0,1:T(2,128)S(1)} %maximum_maximum_fusion.2, f32[2,256,5120]{2,1,0:T(8,128)S(1)} %bitcast.327, pred[256,5120]{1,0:T(8,128)(4,1)S(1)} %bitcast_and_fusion.2, bf16[256,2,64]{0,2,1:T(8,128)(2,1)S(1)} %bitcast.354, ...), kind=kOutput, calls=%fused_computation.14.clone.1 | convolution fusion | flops 351272448 | bytes 23664640 | tf_op jit(solution)/shard_map/while/body/eval_jaxpr/rhe,khe->rhk/dot_general | solution.py:127
  149.5 7.1 %fusion.168 = bf16[256,2,5120]{2,0,1:T(8,128)(2,1)S(1)} fusion(f32[2,256,5120]{2,1,0:T(8,128)} %get-tuple-element.506, f32[256,2]{0,1:T(2,128)S(1)} %add_add_fusion.6, f32[256,2]{0,1:T(2,128)S(1)} %add_add_fusion.5, f32[256,2]{0,1:T(2,128)S(1)} %maximum_maximum_fusion.2, f32[2,256,5120]{2,1,0:T(8,128)S(1)} %bitcast.327, ...), kind=kLoop, calls=%fused_computation.17.clone.1 | loop fusion | flops 20971520 | bytes 27531264 | tf_op jit(solution)/shard_map/while/body/eval_jaxpr/convert_element_type | solution.py:141
  186.8 9.1 %fusion.170 = f32[5120,2,64]{0,2,1:T(8,128)} fusion(bf16[256,2,64]{0,2,1:T(8,128)(2,1)S(1)} %bitcast.353, f32[5120,2,64]{0,2,1:T(8,128)} %get-tuple-element.548, pred[]{:T(512)S(6)} %compare.7, f32[2,256,5120]{2,1,0:T(8,128)} %copy-done.2, f32[256,2]{0,1:T(2,128)S(1)} %add_add_fusion.5, f32[256,2]{0,1:T(2,128)S(1)} %maximum_maximum_fusion.2, ...), kind=kOutput, calls=%fused_computation.25.clone.1 | convolution fusion | flops 349962240 | bytes 17108992 | tf_op jit(solution)/shard_map/while/body/eval_jaxpr/rhk,rhe->khe/dot_general | solution.py:154
  195.9 7.3 %fusion.167 = (f32[256,2]{0,1:T(2,128)S(1)}, f32[2,256,5120]{2,1,0:T(8,128)}) fusion(f32[256,2]{0,1:T(2,128)S(1)} %add_add_fusion.5, f32[256,2]{0,1:T(2,128)S(1)} %maximum_maximum_fusion.2, f32[2,256,5120]{2,1,0:T(8,128)S(1)} %bitcast.327, pred[256,5120]{1,0:T(8,128)(4,1)S(1)} %bitcast_and_fusion.2, bf16[256,2,64]{0,2,1:T(8,128)(2,1)S(1)} %bitcast.354, ...), kind=kOutput, calls=%fused_computation.14.clone.1 | convolution fusion | flops 351272448 | bytes 23664640 | tf_op jit(solution)/shard_map/while/body/eval_jaxpr/rhe,khe->rhk/dot_general | solution.py:127
  203.4 7.1 %fusion.168 = bf16[256,2,5120]{2,0,1:T(8,128)(2,1)S(1)} fusion(f32[2,256,5120]{2,1,0:T(8,128)} %get-tuple-element.506, f32[256,2]{0,1:T(2,128)S(1)} %add_add_fusion.6, f32[256,2]{0,1:T(2,128)S(1)} %add_add_fusion.5, f32[256,2]{0,1:T(2,128)S(1)} %maximum_maximum_fusion.2, f32[2,256,5120]{2,1,0:T(8,128)S(1)} %bitcast.327, ...), kind=kLoop, calls=%fused_computation.17.clone.1 | loop fusion | flops 20971520 | bytes 27531264 | tf_op jit(solution)/shard_map/while/body/eval_jaxpr/convert_element_type | solution.py:141
  240.7 9.1 %fusion.170 = f32[5120,2,64]{0,2,1:T(8,128)} fusion(bf16[256,2,64]{0,2,1:T(8,128)(2,1)S(1)} %bitcast.353, f32[5120,2,64]{0,2,1:T(8,128)} %get-tuple-element.548, pred[]{:T(512)S(6)} %compare.7, f32[2,256,5120]{2,1,0:T(8,128)} %copy-done.2, f32[256,2]{0,1:T(2,128)S(1)} %add_add_fusion.5, f32[256,2]{0,1:T(2,128)S(1)} %maximum_maximum_fusion.2, ...), kind=kOutput, calls=%fused_computation.25.clone.1 | convolution fusion | flops 349962240 | bytes 17108992 | tf_op jit(solution)/shard_map/while/body/eval_jaxpr/rhk,rhe->khe/dot_general | solution.py:154
  249.9 7.3 %fusion.167 = (f32[256,2]{0,1:T(2,128)S(1)}, f32[2,256,5120]{2,1,0:T(8,128)}) fusion(f32[256,2]{0,1:T(2,128)S(1)} %add_add_fusion.5, f32[256,2]{0,1:T(2,128)S(1)} %maximum_maximum_fusion.2, f32[2,256,5120]{2,1,0:T(8,128)S(1)} %bitcast.327, pred[256,5120]{1,0:T(8,128)(4,1)S(1)} %bitcast_and_fusion.2, bf16[256,2,64]{0,2,1:T(8,128)(2,1)S(1)} %bitcast.354, ...), kind=kOutput, calls=%fused_computation.14.clone.1 | convolution fusion | flops 351272448 | bytes 23664640 | tf_op jit(solution)/shard_map/while/body/eval_jaxpr/rhe,khe->rhk/dot_general | solution.py:127
  257.3 7.1 %fusion.168 = bf16[256,2,5120]{2,0,1:T(8,128)(2,1)S(1)} fusion(f32[2,256,5120]{2,1,0:T(8,128)} %get-tuple-element.506, f32[256,2]{0,1:T(2,128)S(1)} %add_add_fusion.6, f32[256,2]{0,1:T(2,128)S(1)} %add_add_fusion.5, f32[256,2]{0,1:T(2,128)S(1)} %maximum_maximum_fusion.2, f32[2,256,5120]{2,1,0:T(8,128)S(1)} %bitcast.327, ...), kind=kLoop, calls=%fused_computation.17.clone.1 | loop fusion | flops 20971520 | bytes 27531264 | tf_op jit(solution)/shard_map/while/body/eval_jaxpr/convert_element_type | solution.py:141
  294.6 9.1 %fusion.170 = f32[5120,2,64]{0,2,1:T(8,128)} fusion(bf16[256,2,64]{0,2,1:T(8,128)(2,1)S(1)} %bitcast.353, f32[5120,2,64]{0,2,1:T(8,128)} %get-tuple-element.548, pred[]{:T(512)S(6)} %compare.7, f32[2,256,5120]{2,1,0:T(8,128)} %copy-done.2, f32[256,2]{0,1:T(2,128)S(1)} %add_add_fusion.5, f32[256,2]{0,1:T(2,128)S(1)} %maximum_maximum_fusion.2, ...), kind=kOutput, calls=%fused_computation.25.clone.1 | convolution fusion | flops 349962240 | bytes 17108992 | tf_op jit(solution)/shard_map/while/body/eval_jaxpr/rhk,rhe->khe/dot_general | solution.py:154
  303.7 7.3 %fusion.167 = (f32[256,2]{0,1:T(2,128)S(1)}, f32[2,256,5120]{2,1,0:T(8,128)}) fusion(f32[256,2]{0,1:T(2,128)S(1)} %add_add_fusion.5, f32[256,2]{0,1:T(2,128)S(1)} %maximum_maximum_fusion.2, f32[2,256,5120]{2,1,0:T(8,128)S(1)} %bitcast.327, pred[256,5120]{1,0:T(8,128)(4,1)S(1)} %bitcast_and_fusion.2, bf16[256,2,64]{0,2,1:T(8,128)(2,1)S(1)} %bitcast.354, ...), kind=kOutput, calls=%fused_computation.14.clone.1 | convolution fusion | flops 351272448 | bytes 23664640 | tf_op jit(solution)/shard_map/while/body/eval_jaxpr/rhe,khe->rhk/dot_general | solution.py:127
  311.2 7.1 %fusion.168 = bf16[256,2,5120]{2,0,1:T(8,128)(2,1)S(1)} fusion(f32[2,256,5120]{2,1,0:T(8,128)} %get-tuple-element.506, f32[256,2]{0,1:T(2,128)S(1)} %add_add_fusion.6, f32[256,2]{0,1:T(2,128)S(1)} %add_add_fusion.5, f32[256,2]{0,1:T(2,128)S(1)} %maximum_maximum_fusion.2, f32[2,256,5120]{2,1,0:T(8,128)S(1)} %bitcast.327, ...), kind=kLoop, calls=%fused_computation.17.clone.1 | loop fusion | flops 20971520 | bytes 27531264 | tf_op jit(solution)/shard_map/while/body/eval_jaxpr/convert_element_type | solution.py:141
  333.6 7.3 %all-to-all-start.1 = ((bf16[32,128,256]{1,2,0:T(8,128)(2,1)}), bf16[32,128,256]{1,2,0:T(8,128)(2,1)}, u32[]{:S(2)}, u32[]{:S(2)}) async-start(bf16[32,128,256]{1,2,0:T(8,128)(2,1)} %copy.119), calls=%async_computation.1 | async-start | bytes 4194304 | tf_op jit(solution)/shard_map/all_to_all | solution.py:185
  344.9 5.5 %scatter_custom_fusion = f32[1024,256]{1,0:T(8,128)S(1)} fusion(s32[1024]{0:T(1024)} %bitcast.373, f32[1024,256]{1,0:T(8,128)} %copy.115, f32[]{:T(128)} %constant.41.clone.1), kind=kCustom, calls=%fused_computation.117 | custom fusion | bytes 1049088 | tf_op jit(solution)/shard_map/scatter | solution.py:203
  353.8 5.5 %scatter_custom_fusion.1 = f32[1024,256]{1,0:T(8,128)S(1)} fusion(s32[1024]{0:T(1024)} %bitcast.371, f32[1024,256]{1,0:T(8,128)} %copy.116, f32[]{:T(128)} %constant.41.clone.1), kind=kCustom, calls=%fused_computation.115 | custom fusion | bytes 1049088 | tf_op jit(solution)/shard_map/scatter | solution.py:203
  361.6 5.5 %scatter_custom_fusion.2 = f32[1024,256]{1,0:T(8,128)S(1)} fusion(s32[1024]{0:T(1024)} %bitcast.369, f32[1024,256]{1,0:T(8,128)} %copy.117, f32[]{:T(128)} %constant.41.clone.1), kind=kCustom, calls=%fused_computation.113 | custom fusion | bytes 1049088 | tf_op jit(solution)/shard_map/scatter | solution.py:203
  390.8 11.4 %collective-permute-done.5 = bf16[1024,256]{1,0:T(8,128)(2,1)} collective-permute-done((bf16[1024,256]{1,0:T(8,128)(2,1)}, bf16[1024,256]{1,0:T(8,128)(2,1)}, u32[]{:S(2)}, u32[]{:S(2)}) %collective-permute-start.5) | collective-permute-done | bytes 524320 | tf_op jit(solution)/shard_map/ppermute | solution.py:13
  408.1 23.4 %scatter_custom_fusion.4 = f32[1024,256]{1,0:T(8,128)S(1)} fusion(f32[1024,256]{1,0:T(8,128)S(1)} %fusion.41, s32[4096]{0:T(1024)S(1)} %bitcast.365, bf16[4096,256]{1,0:T(8,128)(2,1)} %bitcast.336), kind=kCustom, calls=%fused_computation.82 | custom fusion | flops 2097152 | bytes 3145728 | tf_op jit(solution)/shard_map/scatter-add | solution.py:188
  431.5 48.2 %all-reduce.3.cloned.1.call-done = bf16[128,256]{1,0:T(8,128)(2,1)} async-done(((bf16[128,256]{1,0:T(8,128)(2,1)}), bf16[128,256]{1,0:T(8,128)(2,1)}) %all-reduce.3.cloned.1.call-update) | async-done | bytes 65552 | tf_op jit(solution)/shard_map/psum | solution.py:210
  484.2 28.4 %reduce-scatter.2.cloned.1.call-done = f32[1024,128]{1,0:T(8,128)} async-done(((f32[1024,512]{1,0:T(8,128)}), f32[1024,128]{1,0:T(8,128)}) %reduce-scatter.2.cloned.1.call-update) | async-done | bytes 524304 | tf_op jit(solution)/shard_map/reduce_scatter | solution.py:225
  (463 shorter events, 223.7 us)
Async XLA Ops:
  11.1 17.0 %copy-start.14 = (bf16[1024,128]{1,0:T(8,128)(2,1)}, bf16[1024,128]{1,0:T(8,128)(2,1)S(1)}, u32[]{:S(2)}) copy-start(bf16[1024,128]{1,0:T(8,128)(2,1)S(1)} %convolution_convert_fusion) | copy-start | bytes 786436
  28.1 17.5 %copy-start.28 = (s32[4,1024]{1,0:T(4,128)S(1)}, s32[4,1024]{1,0:T(4,128)}, u32[]{:S(2)}) copy-start(s32[4,1024]{1,0:T(4,128)} %param.20) | copy-start | bytes 49156
  28.1 25.1 %copy-start.21 = (bf16[512,128]{1,0:T(8,128)(2,1)S(1)}, bf16[512,128]{1,0:T(8,128)(2,1)}, u32[]{:S(2)}) copy-start(bf16[512,128]{1,0:T(8,128)(2,1)} %param.13) | copy-start | bytes 393220
  28.1 69.3 %all-to-all-start = ((bf16[32,128,256]{2,1,0:T(8,128)(2,1)}), bf16[32,128,256]{2,1,0:T(8,128)(2,1)}, u32[]{:S(2)}, u32[]{:S(2)}) async-start(bf16[32,128,256]{2,1,0:T(8,128)(2,1)} %bitcast.337), calls=%async_computation | async-start | bytes 4194304 | tf_op jit(solution)/shard_map/all_to_all | solution.py:45
  37.7 70.3 %all-gather.2.cloned.1.call-start = ((), (), s32[]{:S(2)}) async-start(), calls=%async_computation.3 | async-start | bytes 2162688 | tf_op jit(solution)/shard_map/all_gather | solution.py:65
  39.9 35.1 %collective-permute-start.3 = (bf16[1024,256]{1,0:T(8,128)(2,1)S(1)}, bf16[1024,256]{1,0:T(8,128)(2,1)}, u32[]{:S(2)}, u32[]{:S(2)}) collective-permute-start(bf16[1024,256]{1,0:T(8,128)(2,1)S(1)} %pad_maximum_fusion.8), channel_id=1, source_target_pairs={{0,32},{4,36},{8,40},{12,44},{16,48},{20,52},{24,56},{28,60},{32,0... | collective-permute-start | bytes 1572872 | tf_op jit(solution)/shard_map/ppermute | solution.py:13
  41.4 38.7 %collective-permute-start.2 = (bf16[1024,256]{1,0:T(8,128)(2,1)S(1)}, bf16[1024,256]{1,0:T(8,128)(2,1)S(1)}, u32[]{:S(2)}, u32[]{:S(2)}) collective-permute-start(bf16[1024,256]{1,0:T(8,128)(2,1)S(1)} %pad_maximum_fusion.8), channel_id=1, source_target_pairs={{0,16},{4,20},{8,24},{12,28},{16,0},{20,4},{24,8},{28,12},{32,48},... | collective-permute-start | bytes 1572872 | tf_op jit(solution)/shard_map/ppermute | solution.py:13
  44.1 42.0 %collective-permute-start.1 = (bf16[1024,256]{1,0:T(8,128)(2,1)S(1)}, bf16[1024,256]{1,0:T(8,128)(2,1)S(1)}, u32[]{:S(2)}, u32[]{:S(2)}) collective-permute-start(bf16[1024,256]{1,0:T(8,128)(2,1)S(1)} %pad_maximum_fusion.8), channel_id=1, source_target_pairs={{0,8},{4,12},{8,0},{12,4},{16,24},{20,28},{24,16},{28,20},{32,40},... | collective-permute-start | bytes 1572872 | tf_op jit(solution)/shard_map/ppermute | solution.py:13
  44.4 46.6 %collective-permute-start = (bf16[1024,256]{1,0:T(8,128)(2,1)S(1)}, bf16[1024,256]{1,0:T(8,128)(2,1)S(1)}, u32[]{:S(2)}, u32[]{:S(2)}) collective-permute-start(bf16[1024,256]{1,0:T(8,128)(2,1)S(1)} %pad_maximum_fusion.8), channel_id=1, source_target_pairs={{0,4},{4,0},{8,12},{12,8},{16,20},{20,16},{24,28},{28,24},{32,36},... | collective-permute-start | bytes 1572872 | tf_op jit(solution)/shard_map/ppermute | solution.py:13
  333.6 70.4 %all-to-all-start.1 = ((bf16[32,128,256]{1,2,0:T(8,128)(2,1)}), bf16[32,128,256]{1,2,0:T(8,128)(2,1)}, u32[]{:S(2)}, u32[]{:S(2)}) async-start(bf16[32,128,256]{1,2,0:T(8,128)(2,1)} %copy.119), calls=%async_computation.1 | async-start | bytes 4194304 | tf_op jit(solution)/shard_map/all_to_all | solution.py:185
  340.9 138.8 %all-reduce.3.cloned.1.call-start = ((), (), s32[]{:S(2)}) async-start(), calls=%async_computation.4 | async-start | bytes 131072 | tf_op jit(solution)/shard_map/psum | solution.py:210
  368.1 12.2 %copy-start.26 = (s32[1,32,128]{2,1,0:T(8,128)S(1)}, s32[1,32,128]{2,1,0:T(8,128)}, u32[]{:S(2)}) copy-start(s32[1,32,128]{2,1,0:T(8,128)} %param.17) | copy-start | bytes 49156
  368.4 14.1 %copy-start.13 = (f32[128,2,64]{0,2,1:T(8,128)S(1)}, f32[128,2,64]{0,2,1:T(8,128)}, u32[]{:S(2)}) copy-start(f32[128,2,64]{0,2,1:T(8,128)} %get-tuple-element.615) | copy-start | bytes 196612
  374.7 13.5 %collective-permute-start.7 = (bf16[1024,256]{1,0:T(8,128)(2,1)}, bf16[1024,256]{1,0:T(8,128)(2,1)}, u32[]{:S(2)}, u32[]{:S(2)}) collective-permute-start(bf16[1024,256]{1,0:T(8,128)(2,1)} %convert_element_type.145), channel_id=1, source_target_pairs={{0,32},{4,36},{8,40},{12,44},{16,48},{20,52},{24,56},{28,60},{32,0... | collective-permute-start | bytes 1572872 | tf_op jit(solution)/shard_map/ppermute | solution.py:13
  376.1 14.7 %collective-permute-start.6 = (bf16[1024,256]{1,0:T(8,128)(2,1)}, bf16[1024,256]{1,0:T(8,128)(2,1)}, u32[]{:S(2)}, u32[]{:S(2)}) collective-permute-start(bf16[1024,256]{1,0:T(8,128)(2,1)} %convert_element_type.143), channel_id=1, source_target_pairs={{0,16},{4,20},{8,24},{12,28},{16,0},{20,4},{24,8},{28,12},{32,48},... | collective-permute-start | bytes 1572872 | tf_op jit(solution)/shard_map/ppermute | solution.py:13
  378.8 23.3 %collective-permute-start.5 = (bf16[1024,256]{1,0:T(8,128)(2,1)}, bf16[1024,256]{1,0:T(8,128)(2,1)}, u32[]{:S(2)}, u32[]{:S(2)}) collective-permute-start(bf16[1024,256]{1,0:T(8,128)(2,1)} %convert_element_type.141), channel_id=1, source_target_pairs={{0,8},{4,12},{8,0},{12,4},{16,24},{20,28},{24,16},{28,20},{32,40},... | collective-permute-start | bytes 1572872 | tf_op jit(solution)/shard_map/ppermute | solution.py:13
  379.1 23.0 %collective-permute-start.4 = (bf16[1024,256]{1,0:T(8,128)(2,1)}, bf16[1024,256]{1,0:T(8,128)(2,1)}, u32[]{:S(2)}, u32[]{:S(2)}) collective-permute-start(bf16[1024,256]{1,0:T(8,128)(2,1)} %convert_element_type.139), channel_id=1, source_target_pairs={{0,4},{4,0},{8,12},{12,8},{16,20},{20,16},{24,28},{28,24},{32,36},... | collective-permute-start | bytes 1572872 | tf_op jit(solution)/shard_map/ppermute | solution.py:13
  384.3 128.4 %reduce-scatter.2.cloned.1.call-start = ((), (), s32[]{:S(2)}) async-start(), calls=%async_computation.5 | async-start | bytes 2621440 | tf_op jit(solution)/shard_map/reduce_scatter | solution.py:225
  386.4 15.7 %copy-start.16 = (f32[1024,128]{1,0:T(8,128)S(1)}, f32[1024,128]{1,0:T(8,128)}, u32[]{:S(2)}) copy-start(f32[1024,128]{1,0:T(8,128)} %copy.110) | copy-start | bytes 1572868
  386.4 15.7 %copy-start.17 = (f32[1024,128]{1,0:T(8,128)S(1)}, f32[1024,128]{1,0:T(8,128)}, u32[]{:S(2)}) copy-start(f32[1024,128]{1,0:T(8,128)} %copy.111) | copy-start | bytes 1572868
  408.1 71.7 %copy-start.34 = (pred[128]{0:T(512)(128)(4,1)S(1)}, pred[128]{0:T(512)(128)(4,1)}, u32[]{:S(2)}) copy-start(pred[128]{0:T(512)(128)(4,1)} %copy-done.33) | copy-start | bytes 388
  408.1 73.8 %copy-start.23 = (bf16[512,128]{1,0:T(8,128)(2,1)S(1)}, bf16[512,128]{1,0:T(8,128)(2,1)}, u32[]{:S(2)}) copy-start(bf16[512,128]{1,0:T(8,128)(2,1)} %param.14) | copy-start | bytes 393220
  431.5 50.8 %copy-start.24 = (bf16[512,128]{1,0:T(8,128)(2,1)S(1)}, bf16[512,128]{1,0:T(8,128)(2,1)}, u32[]{:S(2)}) copy-start(bf16[512,128]{1,0:T(8,128)(2,1)} %param.15) | copy-start | bytes 393220
  482.3 32.1 %copy-start.1 = (bf16[1024,512]{1,0:T(8,128)(2,1)S(1)}, bf16[1024,512]{1,0:T(8,128)(2,1)}, u32[]{:S(2)}) copy-start(bf16[1024,512]{1,0:T(8,128)(2,1)} %param.12) | copy-start | bytes 3145732
  (82 other events, 440.4 us)
Sparse Core Ops, SparseCore 0:
  40.8 57.7 all-gather.1
  384.4 95.2 all-reduce.2
  484.3 28.2 reduce-scatter.1
